TPU v7x, 32 devices: a whole 2x2x4 slice. The times are simulated.
32 devices in a mesh: groups: 2 (over x), seq: 16 (over z, y, core), sub: 1.
Axes of the slice: x: 2, y: 2, z: 4, core: 2. Of those that a mesh axis runs over, the one named last changes fastest.
Arguments:
- hidden_input: bfloat16 [16384, 4096], P(('groups', 'seq')), parts along dimension 0, may hold values from -4 to 4
- norm_gain_vector: bfloat16 [4096], replicated, may hold values from 0.099609375 to 1.8984375
- query_weight: bfloat16 [4096, 2048], P('seq', 'sub'), may hold values from -0.109375 to 0.109375
- key_value_weight: bfloat16 [4096, 2, 512], P('seq', None, 'sub'), may hold values from -0.109375 to 0.109375
- output_weight: bfloat16 [2048, 4096], P('sub', 'seq'), may hold values from -0.125 to 0.125
- adapter_input_down: bfloat16 [32, 4096, 192], P('seq'), may hold values from -0.09375 to 0.09375
- adapter_query_up: bfloat16 [32, 64, 2048], P('seq', None, 'sub'), may hold values from -0.75 to 0.75
- adapter_key_value_up: bfloat16 [32, 2, 64, 512], P('seq', None, None, 'sub'), may hold values from -0.75 to 0.75
- adapter_output_down: bfloat16 [32, 2048, 64], P('seq', 'sub'), may hold values from -0.125 to 0.125
- adapter_output_up: bfloat16 [32, 64, 4096], P('seq', None, 'sub'), may hold values from -0.75 to 0.75
- request_lengths: int32 [8], P('groups'), parts along dimension 0, may hold values from 1 to 4608, 8192 in all
- request_adapter: int32 [8], P('groups'), parts along dimension 0, may hold values from 0 to 31
- adapter_table_slot: int32 [32], replicated, may hold values from 0 to 31, each once
Outputs:
- block_out: bfloat16 [16384, 4096], P(('groups', 'seq'), 'sub'), parts along dimension 0
There are 2 independent parts, one for each index of `groups`. A program takes and returns all parts, laid end to end along the dimension named above; an argument that names none is the same for every part. Nothing has to cross between parts.
Inputs may be any that keep to these rules, and one draw needn't show every extreme that they name: `request_lengths`: the lengths add up to 8192; the longest request has exactly 4608 tokens. `request_adapter`: several requests may name the same adapter. `adapter_table_slot`: each slot holds one adapter.
All inputs are finite; a program needn't handle non-finite values.
Results may differ from a plain program's by a relative error of at most 0.013.
The roundings to bfloat16 on the way count: a program that leaves them out, or rounds other values in their place, can miss the bound.
Values may be sent and summed in bfloat16 or wider, within the bound.
No kernel may reach another device: no remote copies, remote signals or barrier semaphores. Data moves between devices by JAX's collectives and lax.ppermute only.
A program may use at most 448 MiB of HBM per device.

v0:
```python
import jax
import jax.numpy as jnp
from jax import lax
from jax.sharding import PartitionSpec as P

HEAD_WIDTH = 128
WINDOW = 4096
epsilon = 1e-05
adapter_scale = 2.0
rope_base = 10000.0
neg_big = -1e30


def spread(shard, axis, root):
    mine = lax.axis_index(axis) == root
    return lax.psum(jnp.where(mine, shard, jnp.zeros_like(shard)), axis)


def doc_index(positions, doc_ends):
    return jnp.sum((doc_ends[None, :] <= positions[:, None]).astype(jnp.int32), axis=1)


def rotary_apply(heads, request_offsets):
    half_size = heads.shape[-1] // 2
    frequency = rope_base ** (-jnp.arange(half_size, dtype=jnp.float32) * (2.0 / heads.shape[-1]))
    angles = request_offsets.astype(jnp.float32)[:, None] * frequency[None, :]
    cosine = jnp.cos(angles)[:, None, :]
    sine = jnp.sin(angles)[:, None, :]
    first_half = heads[..., :half_size]
    second_half = heads[..., half_size:]
    return jnp.concatenate(
        [first_half * cosine - second_half * sine, second_half * cosine + first_half * sine],
        axis=-1,
    )


def allowed_pairs(query_pos, query_doc, key_pos, doc_ends):
    key_doc = doc_index(key_pos, doc_ends)
    distance = query_pos[:, None] - key_pos[None, :]
    return (
        (query_doc[:, None] == key_doc[None, :])
        & (distance >= 0)
        & (distance < WINDOW)
        & (key_pos[None, :] >= 0)
    )


def shards(
    hidden_input,
    norm_gain_vector,
    query_weight,
    key_value_weight,
    output_weight,
    adapter_input_down,
    adapter_query_up,
    adapter_key_value_up,
    adapter_output_down,
    adapter_output_up,
    request_lengths,
    request_adapter,
    adapter_table_slot,
):
    row_total = hidden_input.shape[0]
    seq_index = lax.axis_index("seq")
    positions = seq_index * row_total + jnp.arange(row_total, dtype=jnp.int32)
    doc_ends = jnp.cumsum(request_lengths)
    doc_ids = doc_index(positions, doc_ends)
    request_count = request_lengths.shape[0]
    member_mask = doc_ids[:, None] == jnp.arange(request_count, dtype=jnp.int32)[None, :]
    begins = doc_ends - request_lengths
    request_offsets = positions - jnp.sum(jnp.where(member_mask, begins[None, :], 0), axis=1)
    widened = hidden_input.astype(jnp.float32)
    normed_hidden = (
        widened
        * lax.rsqrt(jnp.mean(widened * widened, axis=-1, keepdims=True) + epsilon)
        * norm_gain_vector.astype(jnp.float32)
    ).astype(jnp.bfloat16)
    query_cols = query_weight.shape[1]
    kv_cols = key_value_weight.shape[2]
    piece_query = lax.all_gather(query_weight, "seq", axis=0, tiled=True)
    piece_kv = lax.all_gather(key_value_weight, "seq", axis=0, tiled=True)
    query_base_rows = jnp.dot(normed_hidden, piece_query, preferred_element_type=jnp.float32)
    key_value_base = jnp.einsum(
        "td,dck->tck", normed_hidden, piece_kv, preferred_element_type=jnp.float32
    )
    local_total = adapter_input_down.shape[0]
    adapter_rank_size = adapter_input_down.shape[2] // 3
    query_adapter_delta = jnp.zeros((row_total, query_cols), jnp.float32)
    key_adapter_delta = jnp.zeros((row_total, kv_cols), jnp.float32)
    value_adapter_delta = jnp.zeros((row_total, kv_cols), jnp.float32)
    out_adapters = []
    for request_number in range(request_count):
        table_slot = adapter_table_slot[request_adapter[request_number]]
        owner_request = table_slot // local_total
        local_position = table_slot % local_total
        down_weight, up_query, up_kv, out_in, out_up = (
            spread(adapter_input_down[local_position], "seq", owner_request),
            spread(adapter_query_up[local_position], "seq", owner_request),
            spread(adapter_key_value_up[local_position], "seq", owner_request),
            spread(adapter_output_down[local_position], "seq", owner_request),
            spread(adapter_output_up[local_position], "seq", owner_request),
        )
        chosen = member_mask[:, request_number : request_number + 1]
        down_rows = jnp.where(
            chosen, jnp.dot(normed_hidden, down_weight, preferred_element_type=jnp.float32), 0.0
        ).astype(jnp.bfloat16)
        query_adapter_delta = query_adapter_delta + jnp.dot(
            down_rows[:, :adapter_rank_size], up_query, preferred_element_type=jnp.float32
        )
        key_adapter_delta = key_adapter_delta + jnp.dot(
            down_rows[:, adapter_rank_size : 2 * adapter_rank_size],
            up_kv[0],
            preferred_element_type=jnp.float32,
        )
        value_adapter_delta = value_adapter_delta + jnp.dot(
            down_rows[:, 2 * adapter_rank_size :], up_kv[1], preferred_element_type=jnp.float32
        )
        out_adapters.append((out_in, out_up))
    query_head_list = query_cols // HEAD_WIDTH
    key_value_heads = kv_cols // HEAD_WIDTH
    group_width = query_head_list // key_value_heads
    queries = rotary_apply(
        (query_base_rows + adapter_scale * query_adapter_delta).reshape(
            row_total, query_head_list, HEAD_WIDTH
        ),
        request_offsets,
    ).astype(jnp.bfloat16)
    queries = queries.reshape(row_total, key_value_heads, group_width, HEAD_WIDTH)
    key_row_list = rotary_apply(
        (key_value_base[:, 0] + adapter_scale * key_adapter_delta).reshape(
            row_total, key_value_heads, HEAD_WIDTH
        ),
        request_offsets,
    ).astype(jnp.bfloat16)
    value_row_list = (key_value_base[:, 1] + adapter_scale * value_adapter_delta).astype(
        jnp.bfloat16
    )
    kv_rows = jnp.stack([key_row_list.reshape(row_total, kv_cols), value_row_list], axis=1)
    piece = lax.all_gather(kv_rows, "seq", axis=0, tiled=True)
    running_max = jnp.full((key_value_heads, group_width, row_total), neg_big, jnp.float32)
    piece_len = piece.shape[0]
    key_pos = jnp.arange(piece_len, dtype=jnp.int32)
    key_heads = piece[:, 0].reshape(piece_len, key_value_heads, HEAD_WIDTH)
    value_heads = piece[:, 1].reshape(piece_len, key_value_heads, HEAD_WIDTH)
    score_matrix = jnp.einsum(
        "xouc,boc->ouxb", queries, key_heads, preferred_element_type=jnp.float32
    ) * HEAD_WIDTH ** (-0.5)
    allowed = allowed_pairs(positions, doc_ids, key_pos, doc_ends)
    score_matrix = jnp.where(allowed, score_matrix, neg_big)
    new_max = jnp.maximum(running_max, jnp.max(score_matrix, axis=-1))
    weights = jnp.where(allowed, jnp.exp(score_matrix - new_max[..., None]), 0.0)
    running_sum = jnp.sum(weights, axis=-1)
    weighted = jnp.einsum(
        "kgts,skd->kgtd",
        weights.astype(jnp.bfloat16),
        value_heads,
        preferred_element_type=jnp.float32,
    )
    mixed = weighted / running_sum[..., None]
    attended_rows = (
        jnp.transpose(mixed, (2, 0, 1, 3)).reshape(row_total, query_cols).astype(jnp.bfloat16)
    )
    out_sum = jnp.zeros((row_total, adapter_rank_size), jnp.float32)
    for request_number in range(request_count):
        output_product = jnp.dot(
            attended_rows, out_adapters[request_number][0], preferred_element_type=jnp.float32
        )
        out_sum = out_sum + jnp.where(
            member_mask[:, request_number : request_number + 1], output_product, 0.0
        )
    out_down = lax.psum(out_sum.astype(jnp.bfloat16), "sub")
    output_adapter_delta = jnp.zeros((row_total, adapter_output_up.shape[2]), jnp.float32)
    for request_number in range(request_count):
        input_rows = jnp.where(
            member_mask[:, request_number : request_number + 1], out_down, jnp.zeros_like(out_down)
        )
        output_adapter_delta = output_adapter_delta + jnp.dot(
            input_rows, out_adapters[request_number][1], preferred_element_type=jnp.float32
        )
    partial_out = jnp.dot(
        attended_rows,
        lax.all_gather(output_weight, "seq", axis=1, tiled=True),
        preferred_element_type=jnp.float32,
    )
    summed_output = lax.psum_scatter(
        partial_out.astype(jnp.bfloat16), "sub", scatter_dimension=1, tiled=True
    ).astype(jnp.float32)
    return (summed_output + adapter_scale * output_adapter_delta).astype(jnp.bfloat16)


def solution(mesh):
    return jax.shard_map(
        shards,
        mesh=mesh,
        in_specs=(
            P(("groups", "seq"), None),
            P(),
            P("seq", "sub"),
            P("seq", None, "sub"),
            P("sub", "seq"),
            P("seq", None, None),
            P("seq", None, "sub"),
            P("seq", None, None, "sub"),
            P("seq", "sub", None),
            P("seq", None, "sub"),
            P("groups"),
            P("groups"),
            P(),
        ),
        out_specs=P(("groups", "seq"), "sub"),
        check_vma=False,
    )
```

profile of v0, /device:TPU:0, one launch (start us, length us, event | category | flops | bytes accessed | tf_op | source)
XLA Modules:
  0.0 921.7 jit_solution(15412389674003154354)
XLA Ops:
  6.5 1.5 fusion.79
  15.7 1.5 fusion.78
  27.5 3.2 select_bitcast_fusion.4
  30.6 1.0 select_bitcast_fusion.8
  31.6 0.8 select_bitcast_fusion.16
  32.4 2.9 select_bitcast_fusion
  35.3 1.0 select_bitcast_fusion.14
  36.4 1.0 copy-done.11
  37.4 1.2 copy.36
  38.7 0.7 all-gather.9.cloned.1.call-update
  39.9 3.2 fusion.10
  43.2 0.5 multiply_cosine_fusion
  43.7 3.6 fusion.12
  47.4 201.5 %all-reduce.3.cloned.1.call-done = (bf16[64,4096]{1,0:T(8,128)(2,1)}, bf16[2048,64]{0,1:T(8,128)(2,1)}, bf16[2,64,512]{2,1,0:T(8,128)(2,1)}, bf16[4096,192]{0,1:...) async-done(((bf16[64,4096]{1,0:T(8,128)(2,1)}, ...) | async-done | bytes 11010064 | tf_op jit(solution)/shard_map/psum | solution.py:16
  248.8 4.4 fusion.28
  253.9 1.5 fusion.29
  256.2 1.5 fusion.30
  258.5 1.5 fusion.31
  260.1 68.9 %all-gather.5.cloned.1.call-done = bf16[4096,2,512]{0,2,1:T(8,128)(2,1)} async-done(((bf16[256,2,512]{0,2,1:T(8,128)(2,1)}), bf16[4096,2,512]{0,2,1:T(8,128)(2,1)}) %all-gather.5.cloned.1.call-update) | async-done | bytes 8388624 | tf_op jit(solution)/shard_map/all_gather | solution.py:81
  328.9 8.2 fusion.14
  337.2 0.4 fusion.24
  337.8 0.4 fusion.27
  338.2 1.1 pad_maximum_fusion
  340.3 7.0 fusion.9
  347.3 2.7 fusion.36
  350.0 2.7 fusion.38
  352.8 2.7 fusion.42
  355.5 2.7 fusion.40
  358.2 97.6 %all-gather.9.cloned.1.call-done = bf16[4096,2048]{1,0:T(8,128)(2,1)} async-done(((bf16[256,2048]{1,0:T(8,128)(2,1)}), bf16[4096,2048]{1,0:T(8,128)(2,1)}) %all-gather.9.cloned.1.call-update) | async-done | bytes 16777232 | tf_op jit(solution)/shard_map/all_gather | solution.py:80
  455.8 17.9 %add_bitcast_fusion = f32[64,8,16,128]{3,1,2,0:T(8,128)S(1)} fusion(f32[512,2048]{1,0:T(8,128)} %fusion.36, f32[512,2048]{1,0:T(8,128)} %fusion.38, f32[512,2048]{1,0:T(8,128)} %fusion.42, f32[512,2048]{1,0:T(8,128)} %fusion.40, bf16[512,4096]{1,0:T(8,128)(2,1)} %fusion.12, bf16[4096,2048]{1,0:T(8,128)(2,1)} %all-gather.9.cloned.1.call-done), kind=kOutput, calls=%fused_computation.25 | convolution fusion | flops 8595177472 | bytes 41943040 | tf_op jit(solution)/shard_map/dot_general | solution.py:82
  473.6 0.9 copy.56
  474.6 1.6 subtract_convert_fusion
  476.2 0.5 copy.44
  476.7 1.9 copy.43
  478.6 107.3 %all-gather.7.cloned.1.call-done = bf16[8192,2,512]{0,2,1:T(8,128)(2,1)} async-done(((bf16[512,2,512]{0,2,1:T(8,128)(2,1)}), bf16[8192,2,512]{0,2,1:T(8,128)(2,1)}) %all-gather.7.cloned.1.call-update) | async-done | bytes 16777232 | tf_op jit(solution)/shard_map/all_gather | solution.py:139
  585.9 12.2 %fusion.77 = (bf16[8192,1,512]{0,2,1:T(8,128)(2,1)}, bf16[8192,1,512]{0,2,1:T(8,128)(2,1)}) fusion(bf16[8192,2,512]{0,2,1:T(8,128)(2,1)} %all-gather.7.cloned.1.call-done), kind=kLoop, calls=%fused_computation.150 | loop fusion | bytes 33554432 | tf_op jit(solution)/shard_map/slice | solution.py:143
  598.1 99.5 %fusion = (f32[4,4,512]{2,1,0:T(4,128)S(1)}, f32[4,8192,512,4]{2,1,3,0:T(8,128)}) fusion(pred[512,8192]{0,1:T(8,128)(4,1)} %fusion.9, bf16[8192,4,128,1]{0,2,3,1:T(8,128)(2,1)} %bitcast.164, bf16[512,4,4,64]{3,0,2,1:T(8,128)(2,1)S(1)} %bitcast.166, bf16[512,4,4,64]{3,0,2,1:T(8,128)(2,1)} %bitcast.167), kind=kOutput, calls=%fused_computation.2 | convolution fusion | flops 17385381888 | bytes 283148288 | tf_op jit(solution)/shard_map/xouc,boc->ouxb/dot_general | solution.py:145
  697.6 82.0 %fusion.1 = f32[4,4,512]{2,1,0:T(4,128)S(1)} fusion(f32[4,8192,512,4]{2,1,3,0:T(8,128)} %get-tuple-element.66, f32[4,4,512]{2,1,0:T(4,128)S(1)} %broadcast_maximum_fusion, pred[512,8192]{0,1:T(8,128)(4,1)} %fusion.9), kind=kLoop, calls=%fused_computation.3 | loop fusion | flops 335536128 | bytes 272695296 | tf_op jit(solution)/shard_map/reduce_sum | solution.py:152
  779.6 94.6 %fusion.13 = bf16[512,4,4,128]{0,3,2,1:T(8,128)(2,1)S(1)} fusion(bf16[8192,4,128,1]{0,2,3,1:T(8,128)(2,1)} %bitcast.163, f32[4,8192,512,4]{2,1,3,0:T(8,128)} %get-tuple-element.66, f32[4,4,512]{2,1,0:T(4,128)S(1)} %broadcast_maximum_fusion, pred[512,8192]{0,1:T(8,128)(4,1)} %fusion.9, f32[512,4,4]{0,2,1:T(4,128)S(1)} %bitcast.169), kind=kOutput, calls=%fused_computation.20 | convolution fusion | flops 17517510656 | bytes 283181056 | tf_op jit(solution)/shard_map/kgts,skd->kgtd/dot_general | solution.py:153
  874.4 0.5 convolution_select_fusion.7
  874.9 0.5 fusion.34
  875.4 0.5 fusion.33
  875.9 0.5 fusion.35
  876.4 4.6 fusion.55
  880.9 4.5 fusion.59
  885.4 4.5 fusion.57
  890.0 14.3 %convolution_convert_fusion = bf16[512,4096]{1,0:T(8,128)(2,1)} fusion(bf16[512,2048]{0,1:T(8,128)(2,1)S(1)} %bitcast.162, bf16[2048,4096]{1,0:T(8,128)(2,1)} %all-gather.11.cloned.1.call-done), kind=kOutput, calls=%fused_computation.18 | convolution fusion | flops 8592031744 | bytes 23068672 | tf_op jit(solution)/shard_map/dot_general | solution.py:180
  904.3 10.4 %add_convert_fusion = bf16[512,4096]{1,0:T(8,128)(2,1)} fusion(f32[512,4096]{1,0:T(8,128)} %fusion.55, f32[512,4096]{1,0:T(8,128)S(1)} %copy-done, f32[512,4096]{1,0:T(8,128)} %fusion.57, bf16[512,4096]{1,0:T(8,128)(2,1)} %convolution_convert_fusion, bf16[64,4096]{1,0:T(8,128)(2,1)S(1)} %copy-done.7, bf16[512,64]{0,1:T(8,128)(2,1)S(1)} %fusion.35, ...), kind=kOutput, calls=%fused_computation.17 | convolution fusion | flops 283148288 | bytes 34144768 | tf_op jit(solution)/shard_map/dot_general | solution.py:177
  (106 shorter events, 4.0 us)
Async XLA Ops:
  6.5 25.1 %copy-start.6 = (bf16[2,2,64,512]{3,2,1,0:T(8,128)(2,1)S(1)}, bf16[2,2,64,512]{3,2,1,0:T(8,128)(2,1)}, u32[]{:S(2)}) copy-start(bf16[2,2,64,512]{3,2,1,0:T(8,128)(2,1)} %param.20) | copy-start | bytes 786436
  6.5 25.9 %copy-start.2 = (bf16[2,4096,192]{1,2,0:T(8,128)(2,1)S(1)}, bf16[2,4096,192]{1,2,0:T(8,128)(2,1)}, u32[]{:S(2)}) copy-start(bf16[2,4096,192]{1,2,0:T(8,128)(2,1)} %param.18) | copy-start | bytes 9437188
  6.5 242.3 %all-reduce.3.cloned.1.call-start = ((), (), s32[]{:S(2)}) async-start(), calls=%async_computation.4 | async-start | bytes 22020096 | tf_op jit(solution)/shard_map/psum | solution.py:16
  27.4 3.2 copy-start.4
  32.4 2.9 copy-start.5
  36.3 1.0 copy-start.11
  36.3 3.1 copy-start.30
  36.3 3.1 copy-start.36
  36.4 292.6 %all-gather.5.cloned.1.call-start = ((), (), s32[]{:S(2)}) async-start(), calls=%async_computation | async-start | bytes 8912896 | tf_op jit(solution)/shard_map/all_gather | solution.py:81
  38.6 417.1 %all-gather.9.cloned.1.call-start = ((), (), s32[]{:S(2)}) async-start(), calls=%async_computation.2 | async-start | bytes 17825792 | tf_op jit(solution)/shard_map/all_gather | solution.py:80
  39.4 546.5 %all-gather.7.cloned.1.call-start = ((), (), s32[]{:S(2)}) async-start(), calls=%async_computation.1 | async-start | bytes 17825792 | tf_op jit(solution)/shard_map/all_gather | solution.py:139
  39.6 4.1 copy-start.1
  39.8 209.0 %copy-start.26 = (pred[512]{0:T(512)(128)(4,1)}, pred[512]{0:T(512)(128)(4,1)S(1)}, u32[]{:S(2)}) copy-start(pred[512]{0:T(512)(128)(4,1)S(1)} %get-tuple-element.8) | copy-start | bytes 1540
  39.8 214.1 %copy-start.24 = (pred[512]{0:T(512)(128)(4,1)}, pred[512]{0:T(512)(128)(4,1)S(1)}, u32[]{:S(2)}) copy-start(pred[512]{0:T(512)(128)(4,1)S(1)} %get-tuple-element.7) | copy-start | bytes 1540
  39.8 216.4 %copy-start.28 = (pred[512]{0:T(512)(128)(4,1)}, pred[512]{0:T(512)(128)(4,1)S(1)}, u32[]{:S(2)}) copy-start(pred[512]{0:T(512)(128)(4,1)S(1)} %get-tuple-element.6) | copy-start | bytes 1540
  39.8 218.7 %copy-start.31 = (pred[512]{0:T(512)(128)(4,1)}, pred[512]{0:T(512)(128)(4,1)S(1)}, u32[]{:S(2)}) copy-start(pred[512]{0:T(512)(128)(4,1)S(1)} %get-tuple-element.5) | copy-start | bytes 1540
  248.8 4.4 copy-start.23
  248.8 5.1 copy-start.3
  248.8 5.1 copy-start.35
  253.6 1.9 copy-start.22
  253.9 2.3 copy-start.34
  255.8 1.9 copy-start.21
  256.2 2.3 copy-start.33
  260.0 77.1 %copy-start.20 = (bf16[2,64,512]{2,1,0:T(8,128)(2,1)S(1)}, bf16[2,64,512]{2,1,0:T(8,128)(2,1)}, u32[]{:S(2)}) copy-start(bf16[2,64,512]{2,1,0:T(8,128)(2,1)} %get-tuple-element.17) | copy-start | bytes 393220
  338.2 9.1 copy-start.15
  339.3 550.7 %all-gather.11.cloned.1.call-start = ((), (), s32[]{:S(2)}) async-start(), calls=%async_computation.3 | async-start | bytes 17825792 | tf_op jit(solution)/shard_map/all_gather | solution.py:182
  340.3 9.7 %copy-start.14 = (bf16[64,2048]{1,0:T(8,128)(2,1)S(1)}, bf16[64,2048]{1,0:T(8,128)(2,1)}, u32[]{:S(2)}) copy-start(bf16[64,2048]{1,0:T(8,128)(2,1)} %get-tuple-element.20) | copy-start | bytes 786436
  347.3 5.4 copy-start.13
  350.0 5.5 copy-start.12
  779.6 94.7 %copy-start.19 = (bf16[2048,64]{0,1:T(8,128)(2,1)S(1)}, bf16[2048,64]{0,1:T(8,128)(2,1)}, u32[]{:S(2)}) copy-start(bf16[2048,64]{0,1:T(8,128)(2,1)} %get-tuple-element.10) | copy-start | bytes 786436
  779.6 94.7 %copy-start.27 = (pred[512]{0:T(512)(128)(4,1)S(1)}, pred[512]{0:T(512)(128)(4,1)}, u32[]{:S(2)}) copy-start(pred[512]{0:T(512)(128)(4,1)} %copy-done.26) | copy-start | bytes 1540
  779.6 95.2 %copy-start.18 = (bf16[2048,64]{0,1:T(8,128)(2,1)S(1)}, bf16[2048,64]{0,1:T(8,128)(2,1)}, u32[]{:S(2)}) copy-start(bf16[2048,64]{0,1:T(8,128)(2,1)} %get-tuple-element.23) | copy-start | bytes 786436
  779.6 95.2 %copy-start.25 = (pred[512]{0:T(512)(128)(4,1)S(1)}, pred[512]{0:T(512)(128)(4,1)}, u32[]{:S(2)}) copy-start(pred[512]{0:T(512)(128)(4,1)} %copy-done.24) | copy-start | bytes 1540
  874.3 1.1 copy-start.17
  874.3 1.1 copy-start.29
  874.3 1.5 copy-start.16
  874.3 1.5 copy-start.32
  874.8 1.5 copy-start.10
  876.4 4.6 copy-start.9
  880.9 4.5 copy-start.8
  890.0 14.3 %copy-start.7 = (bf16[64,4096]{1,0:T(8,128)(2,1)S(1)}, bf16[64,4096]{1,0:T(8,128)(2,1)}, u32[]{:S(2)}) copy-start(bf16[64,4096]{1,0:T(8,128)(2,1)} %get-tuple-element.28) | copy-start | bytes 1572868
  890.0 14.3 %copy-start = (f32[512,4096]{1,0:T(8,128)S(1)}, f32[512,4096]{1,0:T(8,128)}, u32[]{:S(2)}) copy-start(f32[512,4096]{1,0:T(8,128)} %fusion.59) | copy-start | bytes 25165828
Sparse Core Ops, SparseCore 0:
  36.5 212.3 all-reduce.2
  251.0 77.9 all-gather.4
  331.1 124.5 all-gather.8
  457.8 128.0 all-gather.6
  587.9 128.0 all-gather.10
where the time goes:
time: 932 us; the launch traced here: 922 us
  waiting for transfers between devices  476 us (51%)
  matrix products  283 us (30%)
  other arithmetic  109 us (12%)
  between operations  32.2 us (3%)
  local copies, waits for them, and re-layouts  21.2 us (2%)
    psum x1, waiting for transfers between devices, spread(): return lax.psum(jnp.where(mine, shard, jnp.zeros_like(shard)), axis)  201 us
    all_gather x1, waiting for transfers between devices, shards(): piece = lax.all_gather(kv_rows, 'seq', axis=0, tiled=True)  107 us
    dot_general x1, matrix products, shards(): jnp.einsum('xouc,boc->ouxb', queries, key_heads, preferred_element_type=j...  99.5 us
    all_gather x1, waiting for transfers between devices, shards(): piece_query = lax.all_gather(query_weight, 'seq', axis=0, tiled=True)  97.6 us
    dot_general x1, matrix products, shards(): jnp.einsum('kgts,skd->kgtd', weights.astype(jnp.bfloat16), value_heads, p...  94.6 us
    reduce_sum x1, other arithmetic, shards(): running_sum = jnp.sum(weights, axis=-1)  82 us
    all_gather x1, waiting for transfers between devices, shards(): piece_kv = lax.all_gather(key_value_weight, 'seq', axis=0, tiled=True)  68.9 us
    dot_general x4, matrix products, shards(): jnp.dot(input_rows, out_adapters[request_number][1], preferred_element_ty...  24 us
  transfers between devices with their start and end apart: 5, of which 4 were waited for; matrix products, arithmetic and copies ran while one was open for 41% of the time, Pallas kernels for 0%

commit v1 on v0

--- a/solution.py
+++ b/solution.py
@@ -136,7 +136,25 @@
         jnp.bfloat16
     )
     kv_rows = jnp.stack([key_row_list.reshape(row_total, kv_cols), value_row_list], axis=1)
-    piece = lax.all_gather(kv_rows, "seq", axis=0, tiled=True)
+    w_next = lax.axis_size("seq")
+    state_now = lax.axis_index("seq")
+    newest, b_now, shaped = (w_next, state_now, kv_rows.shape[0])
+    runs = tuple(((p, (p + 1) % newest) for p in range(newest)))
+    series = tuple(((p, (p - 1) % newest) for p in range(newest)))
+    piece = jnp.zeros((*kv_rows.shape[:0], newest * shaped, *kv_rows.shape[1:]), kv_rows.dtype)
+    piece = lax.dynamic_update_slice_in_dim(piece, kv_rows, b_now * shaped, axis=0)
+    later = long_array = kv_rows
+    value_now = newest // 2
+    for ix in range(1, value_now + 1):
+        later = lax.ppermute(later, axis_name="seq", perm=runs)
+        piece = lax.dynamic_update_slice_in_dim(
+            piece, later, (b_now - ix) % newest * shaped, axis=0
+        )
+        if ix < newest - value_now:
+            long_array = lax.ppermute(long_array, perm=series, axis_name="seq")
+            piece = lax.dynamic_update_slice_in_dim(
+                piece, long_array, (b_now + ix) % newest * shaped, axis=0
+            )
     running_max = jnp.full((key_value_heads, group_width, row_total), neg_big, jnp.float32)
     piece_len = piece.shape[0]
     key_pos = jnp.arange(piece_len, dtype=jnp.int32)

time: 932 us -> 974 us (1.045)
  starting transfers between devices: 0.34 us -> 68.3 us
  waiting for transfers between devices: 476 us -> 418 us
  local copies, waits for them, and re-layouts: 21.2 us -> 53.2 us
    ppermute x0 -> x15, waiting for transfers between devices: none -> 147 us  [the longest x8 137 us: shards(): later = lax.ppermute(later, axis_name='seq', perm=runs)]
    all_gather x1 -> x0, waiting for transfers between devices: 107 us -> none  [shards(): piece = lax.all_gather(kv_rows, 'seq', axis=0, tiled=True)]
    all_gather x1, waiting for transfers between devices: 97.6 us -> 0.01 us  [shards(): piece_query = lax.all_gather(query_weight, 'seq', axis=0, tiled=True)]
    ppermute x0 -> x15, starting transfers between devices: none -> 68.2 us  [the longest x8 47.6 us: shards(): later = lax.ppermute(later, axis_name='seq', perm=runs)]
    dynamic_update_slice x0 -> x15, local copies, waits for them, and re-layouts: none -> 22.5 us  [the longest x7 11.5 us: shards(): lax.dynamic_update_slice_in_dim(piece, long_array, (b_now + ix) % newest...]
  transfers between devices with their start and end apart: 5 -> 19, of which waited for: 4 -> 11; matrix products, arithmetic and copies ran while one was open for 41% -> 42% of each run, Pallas kernels for 0% -> 0%
where the time goes in v1:
time: 974 us; the launch traced here: 966 us
  waiting for transfers between devices  418 us (43%)
  matrix products  285 us (29%)
  other arithmetic  109 us (11%)
  starting transfers between devices  68.3 us (7%)
  local copies, waits for them, and re-layouts  53.2 us (5%)
  between operations  32.3 us (3%)
    psum x1, waiting for transfers between devices, spread(): return lax.psum(jnp.where(mine, shard, jnp.zeros_like(shard)), axis)  201 us
    ppermute x8, waiting for transfers between devices, shards(): later = lax.ppermute(later, axis_name='seq', perm=runs)  137 us
    dot_general x1, matrix products, shards(): jnp.einsum('xouc,boc->ouxb', queries, key_heads, preferred_element_type=j...  97.5 us
    dot_general x1, matrix products, shards(): jnp.einsum('kgts,skd->kgtd', weights.astype(jnp.bfloat16), value_heads, p...  94.6 us
    reduce_sum x1, other arithmetic, shards(): running_sum = jnp.sum(weights, axis=-1)  82 us
    all_gather x1, waiting for transfers between devices, shards(): piece_kv = lax.all_gather(key_value_weight, 'seq', axis=0, tiled=True)  68.8 us
    ppermute x8, starting transfers between devices, shards(): later = lax.ppermute(later, axis_name='seq', perm=runs)  47.6 us
    dot_general x4, matrix products, shards(): jnp.dot(input_rows, out_adapters[request_number][1], preferred_element_ty...  24.1 us
  transfers between devices with their start and end apart: 19, of which 11 were waited for; matrix products, arithmetic and copies ran while one was open for 42% of the time, Pallas kernels for 0%

profile of v1, /device:TPU:0, one launch (start us, length us, event | category | flops | bytes accessed | tf_op | source)
XLA Modules:
  0.0 965.7 jit_solution(14827432678623315927)
XLA Ops:
  27.4 3.2 select_bitcast_fusion.4
  32.4 2.9 select_bitcast_fusion
  39.9 3.2 fusion.10
  43.7 3.6 fusion.12
  47.4 201.4 %all-reduce.3.cloned.1.call-done = (bf16[64,4096]{1,0:T(8,128)(2,1)}, bf16[2048,64]{0,1:T(8,128)(2,1)}, bf16[2,64,512]{2,1,0:T(8,128)(2,1)}, bf16[4096,192]{0,1:...) async-done(((bf16[64,4096]{1,0:T(8,128)(2,1)}, ...) | async-done | bytes 11010064 | tf_op jit(solution)/shard_map/psum | solution.py:16
  248.8 4.4 fusion.28
  260.1 68.8 %all-gather.4.cloned.1.call-done = bf16[4096,2,512]{0,2,1:T(8,128)(2,1)} async-done(((bf16[256,2,512]{0,2,1:T(8,128)(2,1)}), bf16[4096,2,512]{0,2,1:T(8,128)(2,1)}) %all-gather.4.cloned.1.call-update) | async-done | bytes 8388624 | tf_op jit(solution)/shard_map/all_gather | solution.py:81
  328.9 8.7 fusion.14
  338.7 6.0 broadcast_in_dim.138
  346.2 4.2 collective-permute-start.1
  350.3 35.1 %collective-permute-done = bf16[512,2,512]{0,2,1:T(8,128)(2,1)S(1)} collective-permute-done((bf16[512,2,512]{0,2,1:T(8,128)(2,1)S(1)}, bf16[512,2,512]{0,2,1:T(8,128)(2,1)S(1)}, u32[]{:S(2)}, u32[]{:S(2)}) %collective-permute-start) | collective-permute-done | bytes 1048608 | tf_op jit(solution)/shard_map/ppermute | solution.py:149
  385.4 4.4 collective-permute-start.3
  389.9 24.4 %collective-permute-done.2 = bf16[512,2,512]{0,2,1:T(8,128)(2,1)S(1)} collective-permute-done((bf16[512,2,512]{0,2,1:T(8,128)(2,1)S(1)}, bf16[512,2,512]{0,2,1:T(8,128)(2,1)S(1)}, u32[]{:S(2)}, u32[]{:S(2)}) %collective-permute-start.2) | collective-permute-done | bytes 1048608 | tf_op jit(solution)/shard_map/ppermute | solution.py:149
  414.3 9.3 collective-permute-done.3
  423.7 4.6 collective-permute-start.5
  428.3 24.9 %collective-permute-done.4 = bf16[512,2,512]{0,2,1:T(8,128)(2,1)S(1)} collective-permute-done((bf16[512,2,512]{0,2,1:T(8,128)(2,1)S(1)}, bf16[512,2,512]{0,2,1:T(8,128)(2,1)S(1)}, u32[]{:S(2)}, u32[]{:S(2)}) %collective-permute-start.4) | collective-permute-done | bytes 1048608 | tf_op jit(solution)/shard_map/ppermute | solution.py:149
  453.2 4.4 collective-permute-start.7
  457.6 12.6 %collective-permute-done.6 = bf16[512,2,512]{0,2,1:T(8,128)(2,1)S(1)} collective-permute-done((bf16[512,2,512]{0,2,1:T(8,128)(2,1)S(1)}, bf16[512,2,512]{0,2,1:T(8,128)(2,1)S(1)}, u32[]{:S(2)}, u32[]{:S(2)}) %collective-permute-start.6) | collective-permute-done | bytes 1048608 | tf_op jit(solution)/shard_map/ppermute | solution.py:149
  470.3 19.5 %collective-permute-start.8 = (bf16[512,2,512]{0,2,1:T(8,128)(2,1)S(1)}, bf16[512,2,512]{0,2,1:T(8,128)(2,1)}, u32[]{:S(2)}, u32[]{:S(2)}) collective-permute-start(bf16[512,2,512]{0,2,1:T(8,128)(2,1)S(1)} %collective-permute-done.6), channel_id=1, source_target_pairs={{0,1},{1,2},{2,3},{3,4},{4,5},{5,6},{6,7},{7,8},{8,9},{9,10},{10,1... | collective-permute-start | bytes 3145736 | tf_op jit(solution)/shard_map/ppermute | solution.py:149
  490.0 7.5 collective-permute-done.8
  497.6 12.0 %collective-permute-start.10 = (bf16[512,2,512]{0,2,1:T(8,128)(2,1)}, bf16[512,2,512]{0,2,1:T(8,128)(2,1)}, u32[]{:S(2)}, u32[]{:S(2)}) collective-permute-start(bf16[512,2,512]{0,2,1:T(8,128)(2,1)} %collective-permute-done.8), channel_id=1, source_target_pairs={{0,1},{1,2},{2,3},{3,4},{4,5},{5,6},{6,7},{7,8},{8,9},{9,10},{10,1... | collective-permute-start | bytes 3145736 | tf_op jit(solution)/shard_map/ppermute | solution.py:149
  509.6 6.9 fusion.9
  518.2 3.9 fusion.36
  522.1 3.6 fusion.38
  525.7 3.6 fusion.42
  530.8 5.3 collective-permute-start.12
  536.1 3.6 fusion.40
  545.2 2.9 collective-permute-start.13
  548.2 2.4 constant_dynamic-update-slice_fusion.9
  550.5 12.5 %collective-permute-done.12 = bf16[512,2,512]{0,2,1:T(8,128)(2,1)S(1)} collective-permute-done((bf16[512,2,512]{0,2,1:T(8,128)(2,1)}, bf16[512,2,512]{0,2,1:T(8,128)(2,1)S(1)}, u32[]{:S(2)}, u32[]{:S(2)}) %collective-permute-start.12) | collective-permute-done | bytes 1048608 | tf_op jit(solution)/shard_map/ppermute | solution.py:149
  563.1 10.5 %collective-permute-start.14 = (bf16[512,2,512]{0,2,1:T(8,128)(2,1)S(1)}, bf16[512,2,512]{0,2,1:T(8,128)(2,1)S(1)}, u32[]{:S(2)}, u32[]{:S(2)}) collective-permute-start(bf16[512,2,512]{0,2,1:T(8,128)(2,1)S(1)} %collective-permute-done.12), channel_id=1, source_target_pairs={{0,1},{1,2},{2,3},{3,4},{4,5},{5,6},{6,7},{7,8},{8,9},{9,10},{10,1... | collective-permute-start | bytes 3145736 | tf_op jit(solution)/shard_map/ppermute | solution.py:149
  574.6 2.3 constant_dynamic-update-slice_fusion.7
  576.9 2.3 constant_dynamic-update-slice_fusion.6
  579.2 2.3 constant_dynamic-update-slice_fusion.5
  581.5 2.3 constant_dynamic-update-slice_fusion.4
  587.0 18.7 %collective-permute-done.14 = bf16[512,2,512]{0,2,1:T(8,128)(2,1)S(1)} collective-permute-done((bf16[512,2,512]{0,2,1:T(8,128)(2,1)S(1)}, bf16[512,2,512]{0,2,1:T(8,128)(2,1)S(1)}, u32[]{:S(2)}, u32[]{:S(2)}) %collective-permute-start.14) | collective-permute-done | bytes 1048608 | tf_op jit(solution)/shard_map/ppermute | solution.py:149
  606.8 14.3 %fusion.77 = (bf16[8192,1,512]{0,2,1:T(8,128)(2,1)}, bf16[8192,1,512]{0,2,1:T(8,128)(2,1)}) fusion(bf16[8192,2,512]{0,2,1:T(8,128)(2,1)} %constant_dynamic-update-slice_fusion), kind=kLoop, calls=%fused_computation.166 | loop fusion | bytes 33554432 | tf_op jit(solution)/shard_map/slice | solution.py:161
  621.1 17.9 %add_bitcast_fusion = f32[64,8,16,128]{3,1,2,0:T(8,128)S(1)} fusion(f32[512,2048]{1,0:T(8,128)} %fusion.36, f32[512,2048]{1,0:T(8,128)} %fusion.38, f32[512,2048]{1,0:T(8,128)} %fusion.42, f32[512,2048]{1,0:T(8,128)} %fusion.40, bf16[512,4096]{1,0:T(8,128)(2,1)} %fusion.12, bf16[4096,2048]{1,0:T(8,128)(2,1)} %all-gather.6.cloned.1.call-done), kind=kOutput, calls=%fused_computation.25 | convolution fusion | flops 8595177472 | bytes 41943040 | tf_op jit(solution)/shard_map/dot_general | solution.py:82
  640.0 1.6 subtract_convert_fusion
  642.1 1.9 copy.30
  644.0 97.5 %fusion = (f32[4,4,512]{2,1,0:T(4,128)S(1)}, f32[4,8192,512,4]{2,1,3,0:T(8,128)}) fusion(pred[512,8192]{0,1:T(8,128)(4,1)} %fusion.9, bf16[8192,4,128,1]{0,2,3,1:T(8,128)(2,1)} %bitcast.164, bf16[512,4,4,64]{3,0,2,1:T(8,128)(2,1)S(1)} %bitcast.166, bf16[512,4,4,64]{3,0,2,1:T(8,128)(2,1)} %bitcast.167), kind=kOutput, calls=%fused_computation.2 | convolution fusion | flops 17385381888 | bytes 283148288 | tf_op jit(solution)/shard_map/xouc,boc->ouxb/dot_general | solution.py:163
  741.5 82.0 %fusion.1 = f32[4,4,512]{2,1,0:T(4,128)S(1)} fusion(f32[4,8192,512,4]{2,1,3,0:T(8,128)} %get-tuple-element.68, f32[4,4,512]{2,1,0:T(4,128)S(1)} %broadcast_maximum_fusion, pred[512,8192]{0,1:T(8,128)(4,1)} %fusion.9), kind=kLoop, calls=%fused_computation.3 | loop fusion | flops 335536128 | bytes 272695296 | tf_op jit(solution)/shard_map/reduce_sum | solution.py:170
  823.5 94.6 %fusion.13 = bf16[512,4,4,128]{0,3,2,1:T(8,128)(2,1)S(1)} fusion(bf16[8192,4,128,1]{0,2,3,1:T(8,128)(2,1)} %bitcast.163, f32[4,8192,512,4]{2,1,3,0:T(8,128)} %get-tuple-element.68, f32[4,4,512]{2,1,0:T(4,128)S(1)} %broadcast_maximum_fusion, pred[512,8192]{0,1:T(8,128)(4,1)} %fusion.9, f32[512,4,4]{0,2,1:T(4,128)S(1)} %bitcast.169), kind=kOutput, calls=%fused_computation.20 | convolution fusion | flops 17517510656 | bytes 283181056 | tf_op jit(solution)/shard_map/kgts,skd->kgtd/dot_general | solution.py:171
  920.2 4.6 fusion.55
  924.8 4.6 fusion.59
  929.4 4.6 fusion.57
  934.0 14.3 %convolution_convert_fusion = bf16[512,4096]{1,0:T(8,128)(2,1)} fusion(bf16[512,2048]{0,1:T(8,128)(2,1)S(1)} %bitcast.162, bf16[2048,4096]{1,0:T(8,128)(2,1)} %all-gather.8.cloned.1.call-done), kind=kOutput, calls=%fused_computation.18 | convolution fusion | flops 8592031744 | bytes 23068672 | tf_op jit(solution)/shard_map/dot_general | solution.py:198
  948.3 10.3 %add_convert_fusion = bf16[512,4096]{1,0:T(8,128)(2,1)} fusion(f32[512,4096]{1,0:T(8,128)} %fusion.55, f32[512,4096]{1,0:T(8,128)S(1)} %copy-done, f32[512,4096]{1,0:T(8,128)} %fusion.57, bf16[512,4096]{1,0:T(8,128)(2,1)} %convolution_convert_fusion, bf16[64,4096]{1,0:T(8,128)(2,1)S(1)} %copy-done.15, bf16[512,64]{0,1:T(8,128)(2,1)S(1)} %fusion.35, ...), kind=kOutput, calls=%fused_computation.17 | convolution fusion | flops 283148288 | bytes 34144768 | tf_op jit(solution)/shard_map/dot_general | solution.py:195
  (171 shorter events, 36.8 us)
Async XLA Ops:
  6.5 25.1 %copy-start.14 = (bf16[2,2,64,512]{3,2,1,0:T(8,128)(2,1)S(1)}, bf16[2,2,64,512]{3,2,1,0:T(8,128)(2,1)}, u32[]{:S(2)}) copy-start(bf16[2,2,64,512]{3,2,1,0:T(8,128)(2,1)} %param.20) | copy-start | bytes 786436
  6.5 25.9 %copy-start.2 = (bf16[2,4096,192]{1,2,0:T(8,128)(2,1)S(1)}, bf16[2,4096,192]{1,2,0:T(8,128)(2,1)}, u32[]{:S(2)}) copy-start(bf16[2,4096,192]{1,2,0:T(8,128)(2,1)} %param.18) | copy-start | bytes 9437188
  6.5 242.3 %all-reduce.3.cloned.1.call-start = ((), (), s32[]{:S(2)}) async-start(), calls=%async_computation.3 | async-start | bytes 22020096 | tf_op jit(solution)/shard_map/psum | solution.py:16
  36.4 292.5 %all-gather.4.cloned.1.call-start = ((), (), s32[]{:S(2)}) async-start(), calls=%async_computation | async-start | bytes 8912896 | tf_op jit(solution)/shard_map/all_gather | solution.py:81
  38.6 582.5 %all-gather.6.cloned.1.call-start = ((), (), s32[]{:S(2)}) async-start(), calls=%async_computation.1 | async-start | bytes 17825792 | tf_op jit(solution)/shard_map/all_gather | solution.py:80
  39.4 894.6 %all-gather.8.cloned.1.call-start = ((), (), s32[]{:S(2)}) async-start(), calls=%async_computation.2 | async-start | bytes 17825792 | tf_op jit(solution)/shard_map/all_gather | solution.py:200
  39.6 4.1 copy-start.1
  39.8 209.0 %copy-start.37 = (pred[512]{0:T(512)(128)(4,1)}, pred[512]{0:T(512)(128)(4,1)S(1)}, u32[]{:S(2)}) copy-start(pred[512]{0:T(512)(128)(4,1)S(1)} %get-tuple-element.8) | copy-start | bytes 1540
  39.8 214.1 %copy-start.35 = (pred[512]{0:T(512)(128)(4,1)}, pred[512]{0:T(512)(128)(4,1)S(1)}, u32[]{:S(2)}) copy-start(pred[512]{0:T(512)(128)(4,1)S(1)} %get-tuple-element.7) | copy-start | bytes 1540
  39.8 216.4 %copy-start.39 = (pred[512]{0:T(512)(128)(4,1)}, pred[512]{0:T(512)(128)(4,1)S(1)}, u32[]{:S(2)}) copy-start(pred[512]{0:T(512)(128)(4,1)S(1)} %get-tuple-element.6) | copy-start | bytes 1540
  39.8 218.7 %copy-start.42 = (pred[512]{0:T(512)(128)(4,1)}, pred[512]{0:T(512)(128)(4,1)S(1)}, u32[]{:S(2)}) copy-start(pred[512]{0:T(512)(128)(4,1)S(1)} %get-tuple-element.5) | copy-start | bytes 1540
  248.8 4.4 copy-start.34
  248.8 5.1 copy-start.3
  248.8 5.1 copy-start.46
  260.1 78.2 %copy-start.30 = (bf16[512,192]{0,1:T(8,128)(2,1)}, bf16[512,192]{0,1:T(8,128)(2,1)S(1)}, u32[]{:S(2)}) copy-start(bf16[512,192]{0,1:T(8,128)(2,1)S(1)} %fusion.31) | copy-start | bytes 589828
  260.1 77.6 %copy-start.31 = (bf16[2,64,512]{2,1,0:T(8,128)(2,1)S(1)}, bf16[2,64,512]{2,1,0:T(8,128)(2,1)}, u32[]{:S(2)}) copy-start(bf16[2,64,512]{2,1,0:T(8,128)(2,1)} %get-tuple-element.17) | copy-start | bytes 393220
  345.9 39.5 %collective-permute-start = (bf16[512,2,512]{0,2,1:T(8,128)(2,1)S(1)}, bf16[512,2,512]{0,2,1:T(8,128)(2,1)S(1)}, u32[]{:S(2)}, u32[]{:S(2)}) collective-permute-start(bf16[512,2,512]{0,2,1:T(8,128)(2,1)S(1)} %get-tuple-element.39), channel_id=1, source_target_pairs={{0,1},{1,2},{2,3},{3,4},{4,5},{5,6},{6,7},{7,8},{8,9},{9,10},{10,1... | collective-permute-start | bytes 3145736 | tf_op jit(solution)/shard_map/ppermute | solution.py:149
  346.2 39.3 %collective-permute-start.1 = (bf16[512,2,512]{0,2,1:T(8,128)(2,1)S(1)}, bf16[512,2,512]{0,2,1:T(8,128)(2,1)S(1)}, u32[]{:S(2)}, u32[]{:S(2)}) collective-permute-start(bf16[512,2,512]{0,2,1:T(8,128)(2,1)S(1)} %get-tuple-element.39), channel_id=1, source_target_pairs={{0,15},{1,0},{2,1},{3,2},{4,3},{5,4},{6,5},{7,6},{8,7},{9,8},{10,9... | collective-permute-start | bytes 3145736 | tf_op jit(solution)/shard_map/ppermute | solution.py:154
  385.4 28.9 %collective-permute-start.2 = (bf16[512,2,512]{0,2,1:T(8,128)(2,1)S(1)}, bf16[512,2,512]{0,2,1:T(8,128)(2,1)S(1)}, u32[]{:S(2)}, u32[]{:S(2)}) collective-permute-start(bf16[512,2,512]{0,2,1:T(8,128)(2,1)S(1)} %collective-permute-done), channel_id=1, source_target_pairs={{0,1},{1,2},{2,3},{3,4},{4,5},{5,6},{6,7},{7,8},{8,9},{9,10},{10,1... | collective-permute-start | bytes 3145736 | tf_op jit(solution)/shard_map/ppermute | solution.py:149
  385.4 38.2 %collective-permute-start.3 = (bf16[512,2,512]{0,2,1:T(8,128)(2,1)S(1)}, bf16[512,2,512]{0,2,1:T(8,128)(2,1)S(1)}, u32[]{:S(2)}, u32[]{:S(2)}) collective-permute-start(bf16[512,2,512]{0,2,1:T(8,128)(2,1)S(1)} %collective-permute-done.1), channel_id=1, source_target_pairs={{0,15},{1,0},{2,1},{3,2},{4,3},{5,4},{6,5},{7,6},{8,7},{9,8},{10,9... | collective-permute-start | bytes 3145736 | tf_op jit(solution)/shard_map/ppermute | solution.py:154
  414.3 55.9 %copy-start.6 = (bf16[512,2,512]{0,2,1:T(8,128)(2,1)}, bf16[512,2,512]{0,2,1:T(8,128)(2,1)S(1)}, u32[]{:S(2)}) copy-start(bf16[512,2,512]{0,2,1:T(8,128)(2,1)S(1)} %collective-permute-done.2) | copy-start | bytes 3145732
  414.3 38.9 %collective-permute-start.4 = (bf16[512,2,512]{0,2,1:T(8,128)(2,1)S(1)}, bf16[512,2,512]{0,2,1:T(8,128)(2,1)S(1)}, u32[]{:S(2)}, u32[]{:S(2)}) collective-permute-start(bf16[512,2,512]{0,2,1:T(8,128)(2,1)S(1)} %collective-permute-done.2), channel_id=1, source_target_pairs={{0,1},{1,2},{2,3},{3,4},{4,5},{5,6},{6,7},{7,8},{8,9},{9,10},{10,1... | collective-permute-start | bytes 3145736 | tf_op jit(solution)/shard_map/ppermute | solution.py:149
  423.7 46.6 %copy-start.8 = (bf16[512,2,512]{0,2,1:T(8,128)(2,1)}, bf16[512,2,512]{0,2,1:T(8,128)(2,1)S(1)}, u32[]{:S(2)}) copy-start(bf16[512,2,512]{0,2,1:T(8,128)(2,1)S(1)} %collective-permute-done.3) | copy-start | bytes 3145732
  423.7 29.5 %collective-permute-start.5 = (bf16[512,2,512]{0,2,1:T(8,128)(2,1)S(1)}, bf16[512,2,512]{0,2,1:T(8,128)(2,1)}, u32[]{:S(2)}, u32[]{:S(2)}) collective-permute-start(bf16[512,2,512]{0,2,1:T(8,128)(2,1)S(1)} %collective-permute-done.3), channel_id=1, source_target_pairs={{0,15},{1,0},{2,1},{3,2},{4,3},{5,4},{6,5},{7,6},{8,7},{9,8},{10,9... | collective-permute-start | bytes 3145736 | tf_op jit(solution)/shard_map/ppermute | solution.py:154
  453.2 17.1 %copy-start.10 = (bf16[512,2,512]{0,2,1:T(8,128)(2,1)}, bf16[512,2,512]{0,2,1:T(8,128)(2,1)S(1)}, u32[]{:S(2)}) copy-start(bf16[512,2,512]{0,2,1:T(8,128)(2,1)S(1)} %collective-permute-done.4) | copy-start | bytes 3145732
  453.2 17.1 %collective-permute-start.6 = (bf16[512,2,512]{0,2,1:T(8,128)(2,1)S(1)}, bf16[512,2,512]{0,2,1:T(8,128)(2,1)S(1)}, u32[]{:S(2)}, u32[]{:S(2)}) collective-permute-start(bf16[512,2,512]{0,2,1:T(8,128)(2,1)S(1)} %collective-permute-done.4), channel_id=1, source_target_pairs={{0,1},{1,2},{2,3},{3,4},{4,5},{5,6},{6,7},{7,8},{8,9},{9,10},{10,1... | collective-permute-start | bytes 3145736 | tf_op jit(solution)/shard_map/ppermute | solution.py:149
  453.2 36.8 %collective-permute-start.7 = (bf16[512,2,512]{0,2,1:T(8,128)(2,1)}, bf16[512,2,512]{0,2,1:T(8,128)(2,1)}, u32[]{:S(2)}, u32[]{:S(2)}) collective-permute-start(bf16[512,2,512]{0,2,1:T(8,128)(2,1)} %collective-permute-done.5), channel_id=1, source_target_pairs={{0,15},{1,0},{2,1},{3,2},{4,3},{5,4},{6,5},{7,6},{8,7},{9,8},{10,9... | collective-permute-start | bytes 3145736 | tf_op jit(solution)/shard_map/ppermute | solution.py:154
  470.3 27.3 %collective-permute-start.8 = (bf16[512,2,512]{0,2,1:T(8,128)(2,1)S(1)}, bf16[512,2,512]{0,2,1:T(8,128)(2,1)}, u32[]{:S(2)}, u32[]{:S(2)}) collective-permute-start(bf16[512,2,512]{0,2,1:T(8,128)(2,1)S(1)} %collective-permute-done.6), channel_id=1, source_target_pairs={{0,1},{1,2},{2,3},{3,4},{4,5},{5,6},{6,7},{7,8},{8,9},{9,10},{10,1... | collective-permute-start | bytes 3145736 | tf_op jit(solution)/shard_map/ppermute | solution.py:149
  490.0 35.7 %collective-permute-start.9 = (bf16[512,2,512]{0,2,1:T(8,128)(2,1)}, bf16[512,2,512]{0,2,1:T(8,128)(2,1)}, u32[]{:S(2)}, u32[]{:S(2)}) collective-permute-start(bf16[512,2,512]{0,2,1:T(8,128)(2,1)} %collective-permute-done.7), channel_id=1, source_target_pairs={{0,15},{1,0},{2,1},{3,2},{4,3},{5,4},{6,5},{7,6},{8,7},{9,8},{10,9... | collective-permute-start | bytes 3145736 | tf_op jit(solution)/shard_map/ppermute | solution.py:154
  497.6 33.2 %collective-permute-start.10 = (bf16[512,2,512]{0,2,1:T(8,128)(2,1)}, bf16[512,2,512]{0,2,1:T(8,128)(2,1)}, u32[]{:S(2)}, u32[]{:S(2)}) collective-permute-start(bf16[512,2,512]{0,2,1:T(8,128)(2,1)} %collective-permute-done.8), channel_id=1, source_target_pairs={{0,1},{1,2},{2,3},{3,4},{4,5},{5,6},{6,7},{7,8},{8,9},{9,10},{10,1... | collective-permute-start | bytes 3145736 | tf_op jit(solution)/shard_map/ppermute | solution.py:149
  518.2 3.9 copy-start.22
  518.2 7.5 copy-start.21
  522.1 14.0 %copy-start.20 = (bf16[64,2048]{1,0:T(8,128)(2,1)S(1)}, bf16[64,2048]{1,0:T(8,128)(2,1)}, u32[]{:S(2)}) copy-start(bf16[64,2048]{1,0:T(8,128)(2,1)} %get-tuple-element.22) | copy-start | bytes 786436
  525.7 19.5 %collective-permute-start.11 = (bf16[512,2,512]{0,2,1:T(8,128)(2,1)}, bf16[512,2,512]{0,2,1:T(8,128)(2,1)S(1)}, u32[]{:S(2)}, u32[]{:S(2)}) collective-permute-start(bf16[512,2,512]{0,2,1:T(8,128)(2,1)} %collective-permute-done.9), channel_id=1, source_target_pairs={{0,15},{1,0},{2,1},{3,2},{4,3},{5,4},{6,5},{7,6},{8,7},{9,8},{10,9... | collective-permute-start | bytes 3145736 | tf_op jit(solution)/shard_map/ppermute | solution.py:154
  530.8 32.3 %collective-permute-start.12 = (bf16[512,2,512]{0,2,1:T(8,128)(2,1)}, bf16[512,2,512]{0,2,1:T(8,128)(2,1)S(1)}, u32[]{:S(2)}, u32[]{:S(2)}) collective-permute-start(bf16[512,2,512]{0,2,1:T(8,128)(2,1)} %collective-permute-done.10), channel_id=1, source_target_pairs={{0,1},{1,2},{2,3},{3,4},{4,5},{5,6},{6,7},{7,8},{8,9},{9,10},{10,1... | collective-permute-start | bytes 3145736 | tf_op jit(solution)/shard_map/ppermute | solution.py:149
  536.1 5.9 copy-start.7
  539.7 3.3 copy-start.9
  539.7 4.5 copy-start.11
  545.2 40.7 %collective-permute-start.13 = (bf16[512,2,512]{0,2,1:T(8,128)(2,1)S(1)}, bf16[512,2,512]{0,2,1:T(8,128)(2,1)S(1)}, u32[]{:S(2)}, u32[]{:S(2)}) collective-permute-start(bf16[512,2,512]{0,2,1:T(8,128)(2,1)S(1)} %collective-permute-done.11), channel_id=1, source_target_pairs={{0,15},{1,0},{2,1},{3,2},{4,3},{5,4},{6,5},{7,6},{8,7},{9,8},{10,9... | collective-permute-start | bytes 3145736 | tf_op jit(solution)/shard_map/ppermute | solution.py:154
  563.1 42.6 %collective-permute-start.14 = (bf16[512,2,512]{0,2,1:T(8,128)(2,1)S(1)}, bf16[512,2,512]{0,2,1:T(8,128)(2,1)S(1)}, u32[]{:S(2)}, u32[]{:S(2)}) collective-permute-start(bf16[512,2,512]{0,2,1:T(8,128)(2,1)S(1)} %collective-permute-done.12), channel_id=1, source_target_pairs={{0,1},{1,2},{2,3},{3,4},{4,5},{5,6},{6,7},{7,8},{8,9},{9,10},{10,1... | collective-permute-start | bytes 3145736 | tf_op jit(solution)/shard_map/ppermute | solution.py:149
  823.5 94.7 %copy-start.26 = (bf16[2048,64]{0,1:T(8,128)(2,1)S(1)}, bf16[2048,64]{0,1:T(8,128)(2,1)}, u32[]{:S(2)}) copy-start(bf16[2048,64]{0,1:T(8,128)(2,1)} %get-tuple-element.10) | copy-start | bytes 786436
  823.5 94.7 %copy-start.38 = (pred[512]{0:T(512)(128)(4,1)S(1)}, pred[512]{0:T(512)(128)(4,1)}, u32[]{:S(2)}) copy-start(pred[512]{0:T(512)(128)(4,1)} %copy-done.37) | copy-start | bytes 1540
  823.5 95.2 %copy-start.25 = (bf16[2048,64]{0,1:T(8,128)(2,1)S(1)}, bf16[2048,64]{0,1:T(8,128)(2,1)}, u32[]{:S(2)}) copy-start(bf16[2048,64]{0,1:T(8,128)(2,1)} %get-tuple-element.23) | copy-start | bytes 786436
  823.5 95.2 %copy-start.36 = (pred[512]{0:T(512)(128)(4,1)S(1)}, pred[512]{0:T(512)(128)(4,1)}, u32[]{:S(2)}) copy-start(pred[512]{0:T(512)(128)(4,1)} %copy-done.35) | copy-start | bytes 1540
  920.2 4.6 copy-start.17
  924.8 4.6 copy-start.16
  934.0 14.3 %copy-start.15 = (bf16[64,4096]{1,0:T(8,128)(2,1)S(1)}, bf16[64,4096]{1,0:T(8,128)(2,1)}, u32[]{:S(2)}) copy-start(bf16[64,4096]{1,0:T(8,128)(2,1)} %get-tuple-element.28) | copy-start | bytes 1572868
  934.0 14.3 %copy-start = (f32[512,4096]{1,0:T(8,128)S(1)}, f32[512,4096]{1,0:T(8,128)}, u32[]{:S(2)}) copy-start(f32[512,4096]{1,0:T(8,128)} %fusion.59) | copy-start | bytes 25165828
  (19 other events, 35.8 us)
Sparse Core Ops, SparseCore 0:
  36.5 212.2 all-reduce.2
  250.9 77.9 all-gather.3
  331.1 194.3 all-gather.5
  527.5 159.3 all-gather.7
